TPU v7x, 256 devices: a whole 4x4x8 slice. The times are simulated.
256 devices in a mesh: tower: 2 (over x_lo), blk: 128 (over z, y, x_hi, core).
Axes of the slice: x: 4 (x_hi: 2, x_lo: 2; x = x_hi * 2 + x_lo), y: 4, z: 8, core: 2. Of those that a mesh axis runs over, the one named last changes fastest.
Arguments:
- pooled: bfloat16 [2, 16384, 1152], P('tower', 'blk'), may hold values from -6 to 6
- final_gain: float32 [2, 1152], P('tower'), may hold values from 0.5 to 1.5
- head_weight: bfloat16 [2, 1152, 1152], P('tower'), may hold values from -0.1875 to 0.1875
- pair_ids: int32 [16384], replicated, may hold values from 0 to 16383
- log_scale: float32 [1], replicated, may hold values from 4.2 to 4.7
- bias: float32 [1], replicated, may hold values from -4 to -1
Outputs:
- emb_grad: float32 [2, 16384, 1152], P('tower', 'blk')
Inputs may be any that keep to these rules, and one draw needn't show every extreme that they name: `pair_ids`: examples with equal ids form positive pairs; every example is a positive pair with its own image and text.
All inputs are finite; a program needn't handle non-finite values.
Results may differ from a plain program's by a relative error of at most 0.0043.
Values may be sent and summed in bfloat16 or wider, within the bound.
A program may use at most 192 MiB of HBM per device.

v0:
```python
import jax
import jax.numpy as jnp
from jax import lax
from jax.sharding import PartitionSpec as P


def partner(value, axis, stride):
    mask = 2**stride
    pairs = [(source, source ^ mask) for source in range(lax.axis_size(axis))]
    return lax.ppermute(value, axis, pairs)


def embed_rows(feats, gain, weight):
    values = feats.astype(jnp.float32)
    center = values - jnp.mean(values, axis=-1, keepdims=True)
    spread = jnp.mean(center * center, axis=-1, keepdims=True)
    normed = (center * lax.rsqrt(spread + 1e-06) * gain).astype(jnp.bfloat16)
    head = jnp.dot(normed, weight, preferred_element_type=jnp.float32)
    length = jnp.sum(head * head, axis=-1, keepdims=True)
    return (head * lax.rsqrt(length + 1e-06)).astype(jnp.bfloat16)


def pair_coef(fixed_rows, moving_rows, fixed_ids, moving_ids, scale, shift):
    logits = (
        scale
        * lax.dot_general(
            fixed_rows, moving_rows, (((1,), (1,)), ((), ())), preferred_element_type=jnp.float32
        )
        + shift
    )
    sign = jnp.where(fixed_ids[:, None] == moving_ids[None, :], jnp.float32(1.0), jnp.float32(-1.0))
    return (-sign * jax.nn.sigmoid(-sign * logits)).astype(jnp.bfloat16)


def pair_forces(fixed_rows, moving_rows, fixed_ids, moving_ids, scale, shift):
    coef = pair_coef(fixed_rows, moving_rows, fixed_ids, moving_ids, scale, shift)
    return jnp.dot(coef, moving_rows, preferred_element_type=jnp.float32)


def on_device(pooled, final_gain, head_weight, pair_ids, log_scale, bias):
    local_embed = embed_rows(pooled[0], final_gain[0], head_weight[0])
    count = local_embed.shape[0]
    scale = jnp.exp(log_scale[0])
    shift = bias[0]
    block_index = lax.axis_index("blk")
    local_ids = lax.dynamic_slice_in_dim(pair_ids, block_index * count, count)
    partner_embed = partner(local_embed, "tower", 0)
    total = pair_forces(
        local_embed,
        lax.all_gather(partner_embed, "blk", axis=0, tiled=True),
        local_ids,
        pair_ids,
        scale,
        shift,
    )
    return total[None]


def solution(mesh):
    placed = (P("tower", "blk", None), P("tower", None), P("tower", None, None), P(), P(), P())
    return jax.shard_map(
        on_device, mesh=mesh, in_specs=placed, out_specs=P("tower", "blk", None), check_vma=False
    )
```

profile of v0, /device:TPU:2, one launch (start us, length us, event | category | flops | bytes accessed | tf_op | source)
XLA Modules:
  0.0 294.3 jit_solution(8610071853615321268)
XLA Ops:
  6.5 0.0 copy-start
  6.5 0.0 all-gather.2.cloned.1.call-start
  6.5 1.2 convert_reduce_fusion
  7.8 1.2 fusion.23
  9.0 0.7 reduce.1
  9.7 0.0 copy-done
  9.7 1.7 multiply_reduce_fusion
  11.4 0.1 multiply_convert_fusion
  11.5 2.3 collective-permute-start
  13.9 6.5 %collective-permute-done = bf16[128,1152]{1,0:T(8,128)(2,1)S(1)} collective-permute-done((bf16[128,1152]{1,0:T(8,128)(2,1)S(1)}, bf16[128,1152]{1,0:T(8,128)(2,1)S(1)}, u32[]{:S(2)}, u32[]{:S(2)}) %collective-permute-start) | collective-permute-done | bytes 294944 | tf_op jit(solution)/shard_map/ppermute | solution.py:10
  20.4 0.0 copy-start.1
  20.4 0.7 copy-done.1
  21.1 0.0 all-gather.2.cloned.1.call-update
  22.4 0.8 dynamic_slice.3
  23.2 227.8 %all-gather.2.cloned.1.call-done = bf16[16384,1152]{1,0:T(8,128)(2,1)} async-done(((bf16[128,1152]{1,0:T(8,128)(2,1)}), bf16[16384,1152]{1,0:T(8,128)(2,1)}) %all-gather.2.cloned.1.call-update) | async-done | bytes 37748752 | tf_op jit(solution)/shard_map/all_gather | solution.py:50
  251.0 36.4 %fusion.17 = f32[1,128,1152]{2,1,0:T(8,128)} fusion(bf16[16384,1152]{1,0:T(8,128)(2,1)} %all-gather.2.cloned.1.call-done, bf16[128,1152]{1,0:T(8,128)(2,1)S(1)} %multiply_convert_fusion, f32[]{:T(128)} %bitcast.25, f32[]{:T(128)} %bitcast, s32[16384]{0:T(1024)} %param.9, s32[128]{0:T(128)S(1)} %dynamic_slice.3), kind=kOutput, calls=%fused_computation.18 | convolution fusion | flops 9686745088 | bytes 38699528 | tf_op jit(solution)/shard_map/dot_general | solution.py:37
  (3 shorter events, 0.0 us)
Async XLA Ops:
  6.5 3.2 %copy-start = (bf16[1,1152,1152]{2,1,0:T(8,128)(2,1)S(1)}, bf16[1,1152,1152]{2,1,0:T(8,128)(2,1)}, u32[]{:S(2)}) copy-start(bf16[1,1152,1152]{2,1,0:T(8,128)(2,1)} %param.8) | copy-start | bytes 7962628
  6.5 244.5 %all-gather.2.cloned.1.call-start = ((), (), s32[]{:S(2)}) async-start(), calls=%async_computation | async-start | bytes 38043648 | tf_op jit(solution)/shard_map/all_gather | solution.py:50
  11.5 8.8 %collective-permute-start = (bf16[128,1152]{1,0:T(8,128)(2,1)S(1)}, bf16[128,1152]{1,0:T(8,128)(2,1)S(1)}, u32[]{:S(2)}, u32[]{:S(2)}) collective-permute-start(bf16[128,1152]{1,0:T(8,128)(2,1)S(1)} %multiply_convert_fusion), channel_id=1, source_target_pairs={{0,128},{128,0},{1,129},{129,1},{2,130},{130,2},{3,131},{131,3},{4... | collective-permute-start | bytes 884744 | tf_op jit(solution)/shard_map/ppermute | solution.py:10
  20.4 0.7 copy-start.1
Sparse Core Ops, SparseCore 0:
  21.2 229.7 all-gather.1
where the time goes:
time: 297 us; the launch traced here: 294 us
  waiting for transfers between devices  234 us (79%)
  matrix products  38.1 us (13%)
  between operations  14.8 us (5%)
  other arithmetic  3.27 us (1%)
    all_gather x1, waiting for transfers between devices, on_device(): lax.all_gather(partner_embed, 'blk', axis=0, tiled=True)  228 us
    dot_general x1, matrix products, pair_forces(): return jnp.dot(coef, moving_rows, preferred_element_type=jnp.float32)  36.4 us
    ppermute x1, waiting for transfers between devices, partner(): return lax.ppermute(value, axis, pairs)  6.51 us
  transfers between devices with their start and end apart: 2, of which 2 were waited for; matrix products, arithmetic and copies ran while one was open for 0% of the time, Pallas kernels for 0%

commit v1 on v0

v1 whole, which is shorter than its diff:
```python
import jax
import jax.numpy as jnp
from jax import lax
from jax.experimental import pallas as pl
from jax.experimental.pallas import tpu as pltpu
from jax.sharding import PartitionSpec as P

MESH = pl.DeviceIdType.MESH
BF = jnp.bfloat16
F32 = jnp.float32

Y_SLOT = {2: 0, 0: 1, 1: 2, -1: 3}
Z_SLOT = {4: 0, 3: 1, -3: 2, 2: 3, -2: 4, 1: 5, -1: 6, 0: 7}
UNITS = ((0, 384), (384, 256), (640, 384))
Z_OUT = ((0, 1), (1, 1), (0, 2), (1, 2), (0, 3), (1, 3), (0, 4))
Z_BACK = ((0, 4), (1, 3), (0, 3), (1, 2), (0, 2), (1, 1), (0, 1))


def kernel(
    pooled, gain, weight, ids, log_scale, bias, out,
    w_buf, emb, img, txt, coef, g_img, g_txt, s_img, s_x, s_txt, r_sib, r_z, r_y2, r_y1, r_x, r_fin,
    img_ids, txt_ids,
    w_sem, sx, rx, stx, rtx, sy, ry, sz, rz, ss, rs, ss2, rs2, szr, rzr, syr, ryr, sxr, rxr, sf, rf,
):
    t = lax.axis_index("tower")
    b = lax.axis_index("blk")
    c = lax.rem(b, 2)
    h = lax.rem(b // 2, 2)
    y = lax.rem(b // 4, 4)
    z = b // 16
    x = h * 2 + t
    is_img = t == 0
    is_txt = t == 1
    home = c == t
    guest = c != t

    def at(dx=0, dy=0, dz=0, dc=0):
        nx = lax.rem(x + dx + 4, 4)
        ny = lax.rem(y + dy + 4, 4)
        nz = lax.rem(z + dz + 8, 8)
        nc = lax.rem(c + dc, 2)
        return (lax.rem(nx, 2), ((nz * 4 + ny) * 2 + nx // 2) * 2 + nc)

    xp, xm, x2 = at(dx=1), at(dx=-1), at(dx=2)
    yd = (at(dy=1), at(dy=-1))
    zd = (at(dz=1), at(dz=-1))
    sib = at(dc=1)

    barrier = pltpu.get_barrier_semaphore()
    for peer in (xp, xm, x2, yd[0], yd[1], zd[0], zd[1], sib):
        pl.semaphore_signal(barrier, 1, device_id=peer, device_id_type=MESH)

    fetch = pltpu.make_async_copy(weight.at[0], w_buf, w_sem)
    fetch.start()

    def move(src, dst, send, recv, peer):
        return pltpu.make_async_remote_copy(
            src_ref=src, dst_ref=dst, send_sem=send, recv_sem=recv, device_id=peer, device_id_type=MESH
        )

    def rows(start, n=64):
        return pl.ds(start, n)

    def i_row(rel, q, half):
        return Y_SLOT[rel] * 256 + q * 128 + half * 64

    def t_row(rel, half):
        return Z_SLOT[rel] * 128 + half * 64

    values = pooled[0].astype(F32)
    center = values - jnp.mean(values, axis=-1, keepdims=True)
    spread = jnp.mean(center * center, axis=-1, keepdims=True)
    normed = (center * lax.rsqrt(spread + 1e-06) * gain[...]).astype(BF)
    fetch.wait()
    head = jnp.dot(normed, w_buf[...], preferred_element_type=F32)
    length = jnp.sum(head * head, axis=-1, keepdims=True)
    emb[...] = (head * lax.rsqrt(length + 1e-06)).astype(BF)
    pl.semaphore_wait(barrier, 8)

    def x_copies():
        res = []
        for half in (0, 1):
            for k, (peer, q) in enumerate(((xp, 0), (xm, 1), (x2, 1))):
                dst = img.at[rows(i_row(0, q, half))]
                res.append(move(emb.at[rows(half * 64)], dst, sx.at[k, half], rx.at[q, half], peer))
        return res

    def x_wait(q, half):
        dst = img.at[rows(i_row(0, q, half))]
        move(emb.at[rows(half * 64)], dst, sx.at[0, half], rx.at[q, half], xp).wait_recv()

    def tx_copies():
        return [
            move(emb.at[rows(half * 64)], txt.at[rows(t_row(0, half))], stx.at[half], rtx.at[half], xm)
            for half in (0, 1)
        ]

    def y_copy(d, q, half, dist):
        sign = 1 - 2 * d
        idx = q * 2 + half if dist == 1 else 4 + q
        src_rel = 0 if dist == 1 else -sign
        dst_rel = -sign if dist == 1 else 2
        return move(
            img.at[rows(i_row(src_rel, q, half))], img.at[rows(i_row(dst_rel, q, half))],
            sy.at[d, idx], ry.at[d, idx], yd[d],
        )

    def z_rel(d, dist):
        rel = -dist if d == 0 else dist
        return 4 if rel == -4 else rel

    def z_copy(d, i):
        half, dist = Z_OUT[i]
        half = half ^ d
        src = txt.at[rows(t_row(z_rel(d, dist - 1), half))]
        dst = txt.at[rows(t_row(z_rel(d, dist), half))]
        return move(src, dst, sz.at[d, i], rz.at[d, i], zd[d])

    def s_copy(n, rel, half):
        part = txt.at[rows(t_row(rel, half))]
        return move(part, part, ss.at[n], rs.at[n], sib)

    S_LIST = [(0, 0), (0, 1)] + [(z_rel(d, Z_OUT[i][1]), Z_OUT[i][0] ^ d) for i in range(7) for d in (0, 1)]

    @pl.when(is_img)
    def _():
        for copy in x_copies():
            copy.start()
        img[256:384, :] = emb[...]

    @pl.when(jnp.logical_and(is_txt, guest))
    def _():
        for copy in tx_copies():
            copy.start()

    @pl.when(jnp.logical_and(is_txt, home))
    def _():
        txt[896:1024, :] = emb[...]

    def z_own():
        for i in (0, 1):
            for d in (0, 1):
                z_copy(d, i).start()
        for n in (0, 1):
            s_copy(n, *S_LIST[n]).start()

    @pl.when(jnp.logical_and(is_txt, home))
    def _():
        z_own()

    @pl.when(is_txt)
    def _():
        x_wait(0, 0)
        x_wait(0, 1)

    y_copy(0, 0, 0, 1).start()
    y_copy(1, 0, 1, 1).start()

    for rel, slot in Z_SLOT.items():
        row = ((lax.rem(z + rel + 8, 8) * 4 + y) * 2 + h) * 2 + t
        txt_ids[:, slot * 128 : slot * 128 + 128] = jnp.broadcast_to(ids[pl.ds(row, 1), :], (8, 128))
    for rel, slot in Y_SLOT.items():
        for q in (0, 1):
            row = ((z * 4 + lax.rem(y + rel + 4, 4)) * 2 + lax.rem(h + q, 2)) * 2 + c
            block = jnp.broadcast_to(ids[pl.ds(row, 1), :], (128, 128))
            start = slot * 256 + q * 128
            img_ids[start : start + 128, :] = block.T

    @pl.when(jnp.logical_and(is_img, home))
    def _():
        for copy in tx_copies():
            copy.wait_recv()
        z_own()

    x_wait(1, 0)
    x_wait(1, 1)
    y_copy(0, 1, 0, 1).start()
    y_copy(1, 1, 1, 1).start()

    def z_step(i):
        for d in (0, 1):
            z_copy(d, i).wait_recv()
            if i + 2 < 7:
                z_copy(d, i + 2).start()
            n = 2 + i * 2 + d
            s_copy(n, *S_LIST[n]).start()

    def z_steps(*steps):
        @pl.when(home)
        def _():
            for i in steps:
                z_step(i)

    def y_relay(q):
        for d in (0, 1):
            y_copy(d, q, d, 1).wait_recv()
            y_copy(d, q, d, 2).start()

    z_steps(0, 1)
    y_relay(0)
    z_steps(2)
    y_relay(1)
    for q in (0, 1):
        for d in (0, 1):
            y_copy(d, q, 1 - d, 1).start()
    z_steps(3, 4, 5, 6)

    @pl.when(guest)
    def _():
        for n in range(16):
            s_copy(n, *S_LIST[n]).wait_recv()

    scale = jnp.exp(log_scale[...])
    shift = bias[...]

    def tile(slot):
        part = pl.ds(slot * 256, 256)
        logits = scale * lax.dot_general(
            img[part, :], txt[...], (((1,), (1,)), ((), ())), preferred_element_type=F32
        ) + shift
        same = img_ids[part, 0:1] == txt_ids[0:1, :]
        weight_ = 1.0 / (1.0 + jnp.exp(jnp.minimum(jnp.where(same, logits, -logits), 88.0)))
        coef[part, :] = jnp.where(same, -weight_, weight_).astype(BF)
        g_img[part, :] = jnp.dot(coef[part, :], txt[...], preferred_element_type=F32)

    def yr_copy(d, q, half, dist):
        sign = 1 - 2 * d
        if dist == 2:
            return move(
                s_img.at[rows(i_row(2, q, half))], r_y2.at[rows((d * 2 + q) * 64)],
                syr.at[d, 4 + q], ryr.at[d, 4 + q], yd[d],
            )
        idx = q * 2 + half
        return move(
            s_img.at[rows(i_row(sign, q, half))], r_y1.at[rows((d * 4 + idx) * 64)],
            syr.at[d, idx], ryr.at[d, idx], yd[d],
        )

    for d in (0, 1):
        for q in (0, 1):
            y_copy(d, q, d, 2).wait_recv()
    tile(0)
    s_img[0:256, :] = g_img[0:256, :].astype(BF)
    for q in (0, 1):
        for d in (0, 1):
            yr_copy(d, q, d, 2).start()
    tile(1)

    def first_units():
        g_txt[...] = lax.dot_general(
            coef[0:512, :], img[0:512, :], (((0,), (0,)), ((), ())), preferred_element_type=F32
        )

    first_units()

    def y_side(d):
        sign = 1 - 2 * d
        slot = Y_SLOT[sign]
        tile(slot)
        for q in (0, 1):
            yr_copy(d, q, d, 2).wait_recv()
            for half in (0, 1):
                start = i_row(sign, q, half)
                total = g_img[start : start + 64, :]
                if half == d:
                    total = total + r_y2[(d * 2 + q) * 64 : (d * 2 + q) * 64 + 64, :].astype(F32)
                s_img[start : start + 64, :] = total.astype(BF)
                yr_copy(d, q, half, 1).start()

    for d in (0, 1):
        for q in (0, 1):
            y_copy(d, q, 1 - d, 1).wait_recv()
    y_side(0)
    y_side(1)

    def s2_copy(u):
        part = pl.ds(*UNITS[u])
        return move(s_txt.at[part], r_sib.at[part], ss2.at[u], rs2.at[u], sib)

    for u, (start, n) in enumerate(UNITS):
        g_txt[start : start + n, :] += lax.dot_general(
            coef[512:1024, start : start + n], img[512:1024, :], (((0,), (0,)), ((), ())), preferred_element_type=F32
        )

        @pl.when(guest)
        def _():
            s_txt[start : start + n, :] = g_txt[start : start + n, :].astype(BF)
            s2_copy(u).start()

    def zr_copy(d, i):
        half, dist = Z_BACK[i]
        half = half ^ d
        rel = dist if d == 0 else -dist
        rel = 4 if rel == -4 else rel
        return move(
            s_txt.at[rows(t_row(rel, half))], r_z.at[rows((d * 7 + i) * 64)], szr.at[d, i], rzr.at[d, i], zd[d]
        )

    def zr_take(d, i):
        zr_copy(d, i - 2).wait_recv()
        return r_z[(d * 7 + i - 2) * 64 : (d * 7 + i - 2) * 64 + 64, :].astype(F32)

    def zr_send(i):
        for d in (0, 1):
            half, dist = Z_BACK[i]
            half = half ^ d
            rel = dist if d == 0 else -dist
            start = t_row(4 if rel == -4 else rel, half)
            total = g_txt[start : start + 64, :] + r_sib[start : start + 64, :].astype(F32)
            if i >= 2:
                total = total + zr_take(d, i)
            s_txt[start : start + 64, :] = total.astype(BF)
            zr_copy(d, i).start()

    def xr_copies(q, half):
        src = s_x.at[rows(q * 128 + half * 64)]
        if q == 0:
            return [(is_txt, move(src, r_x.at[rows(half * 64)], sxr.at[q, half], rxr.at[0, half], xm))]
        return [
            (is_txt, move(src, r_x.at[rows(128 + half * 64)], sxr.at[q, half], rxr.at[1, half], xp)),
            (is_img, move(src, r_x.at[rows(256 + half * 64)], sxr.at[q, half], rxr.at[2, half], x2)),
        ]

    def y_final(q, half):
        for d in (0, 1):
            yr_copy(d, q, half, 1).wait_recv()
        start = i_row(0, q, half)
        k = (q * 2 + half) * 64
        total = g_img[start : start + 64, :] + r_y1[k : k + 64, :].astype(F32) + r_y1[256 + k : 256 + k + 64, :].astype(F32)
        if q == 0:
            g_img[start : start + 64, :] = total
        s_x[q * 128 + half * 64 : q * 128 + half * 64 + 64, :] = total.astype(BF)
        for cond, copy in xr_copies(q, half):
            pl.when(cond)(copy.start)

    def zr_steps(*steps):
        @pl.when(home)
        def _():
            for i in steps:
                zr_send(i)

    @pl.when(home)
    def _():
        s2_copy(0).wait_recv()

    zr_steps(0, 1)

    @pl.when(home)
    def _():
        s2_copy(1).wait_recv()
        s2_copy(2).wait_recv()

    zr_steps(2)
    y_final(0, 0)
    zr_steps(3)
    y_final(0, 1)
    zr_steps(4)
    y_final(1, 0)
    zr_steps(5)
    y_final(1, 1)
    zr_steps(6)

    def f_copies():
        return [
            move(s_txt.at[rows(896 + half * 64)], r_fin.at[rows(half * 64)], sf.at[half], rf.at[half], xp)
            for half in (0, 1)
        ]

    @pl.when(home)
    def _():
        for half in (1, 0):
            start = t_row(0, half)
            total = g_txt[start : start + 64, :] + r_sib[start : start + 64, :].astype(F32)
            for d in (0, 1):
                i = 7 if half ^ d == 1 else 8
                total = total + zr_take(d, i)

            @pl.when(is_txt)
            def _():
                out[0, half * 64 : half * 64 + 64, :] = total

            @pl.when(is_img)
            def _():
                s_txt[start : start + 64, :] = total.astype(BF)
                f_copies()[half].start()

    @pl.when(is_img)
    def _():
        for half in (0, 1):
            for k in range(3):
                part = r_x.at[rows(k * 128 + half * 64)]
                move(part, part, sxr.at[0, half], rxr.at[k, half], xp).wait_recv()
            total = g_img[i_row(0, 0, half) : i_row(0, 0, half) + 64, :]
            for k in range(3):
                total = total + r_x[k * 128 + half * 64 : k * 128 + half * 64 + 64, :].astype(F32)
            out[0, half * 64 : half * 64 + 64, :] = total

    @pl.when(jnp.logical_and(is_txt, guest))
    def _():
        for copy in f_copies():
            copy.wait_recv()
        out[0, :, :] = r_fin[...].astype(F32)

    @pl.when(is_img)
    def _():
        for copy in x_copies():
            copy.wait_send()

    @pl.when(jnp.logical_and(is_txt, guest))
    def _():
        for copy in tx_copies():
            copy.wait_send()

    for d in (0, 1):
        for q in (0, 1):
            for half in (0, 1):
                y_copy(d, q, half, 1).wait_send()
                yr_copy(d, q, half, 1).wait_send()
            y_copy(d, q, d, 2).wait_send()
            yr_copy(d, q, d, 2).wait_send()

    @pl.when(home)
    def _():
        for i in range(7):
            for d in (0, 1):
                z_copy(d, i).wait_send()
                zr_copy(d, i).wait_send()
        for n in range(16):
            s_copy(n, *S_LIST[n]).wait_send()

    @pl.when(guest)
    def _():
        for u in range(3):
            s2_copy(u).wait_send()

    for q in (0, 1):
        for half in (0, 1):
            for cond, copy in xr_copies(q, half):
                pl.when(cond)(copy.wait_send)

    @pl.when(jnp.logical_and(is_img, home))
    def _():
        for copy in f_copies():
            copy.wait_send()


def on_device(pooled, final_gain, head_weight, pair_ids, log_scale, bias):
    n, d = pooled.shape[1:]
    vmem = pl.BlockSpec(memory_space=pltpu.VMEM)
    buf = lambda r, kind=BF: pltpu.VMEM((r, d), kind)
    dma = pltpu.SemaphoreType.DMA
    return pl.pallas_call(
        kernel,
        out_shape=jax.ShapeDtypeStruct((1, n, d), F32),
        in_specs=[vmem, vmem, pl.BlockSpec(memory_space=pl.ANY), vmem, vmem, vmem],
        out_specs=vmem,
        scratch_shapes=[
            buf(d), buf(128), buf(1024), buf(1024), pltpu.VMEM((1024, 1024), BF), buf(1024, F32), buf(1024, F32),
            buf(1024), buf(256), buf(1024), buf(1024), buf(14 * 64), buf(4 * 64), buf(8 * 64), buf(6 * 64), buf(128),
            pltpu.VMEM((1024, 128), jnp.int32), pltpu.VMEM((8, 1024), jnp.int32),
            dma, dma((3, 2)), dma((2, 2)), dma((2,)), dma((2,)), dma((2, 6)), dma((2, 6)), dma((2, 7)), dma((2, 7)),
            dma((16,)), dma((16,)), dma((3,)), dma((3,)), dma((2, 7)), dma((2, 7)), dma((2, 6)), dma((2, 6)),
            dma((2, 2)), dma((3, 2)), dma((2,)), dma((2,)),
        ],
        compiler_params=pltpu.CompilerParams(collective_id=0, has_side_effects=True, vmem_limit_bytes=60 * 2**20),
        name="towers",
    )(pooled, final_gain, head_weight, pair_ids.reshape(128, 128), log_scale.reshape(1, 1), bias.reshape(1, 1))


def solution(mesh):
    placed = (P("tower", "blk", None), P("tower", None), P("tower", None, None), P(), P(), P())
    return jax.shard_map(
        on_device, mesh=mesh, in_specs=placed, out_specs=P("tower", "blk", None), check_vma=False
    )
```

time: 297 us -> 84.4 us (0.28)
  waiting for transfers between devices: 234 us -> 0 us
  Pallas kernels: 0 us -> 81 us
  matrix products: 38.1 us -> 0 us
  between operations: 14.8 us -> 1.3 us
  other arithmetic: 3.27 us -> 0 us
    all_gather x1 -> x0, waiting for transfers between devices: 228 us -> none  [on_device(): lax.all_gather(partner_embed, 'blk', axis=0, tiled=True)]
    pallas_call x0 -> x1, Pallas kernels: none -> 81 us  [on_device(): pl.pallas_call(kernel, out_shape=jax.ShapeDtypeStruct((1, n, d), F32), in...]
    dot_general x2 -> x0, matrix products: 38.1 us -> none  [the longest x1 36.4 us: pair_forces(): return jnp.dot(coef, moving_rows, preferred_element_type=jnp.float32)]
    ppermute x1 -> x0, waiting for transfers between devices: 6.51 us -> none  [partner(): return lax.ppermute(value, axis, pairs)]
  transfers between devices with their start and end apart: 2 -> 0, of which waited for: 2 -> 0; matrix products, arithmetic and copies ran while one was open for 0% -> 0% of each run, Pallas kernels for 0% -> 0%
where the time goes in v1:
time: 84.4 us; the launch traced here: 84.2 us
  Pallas kernels  81 us (96%)
  local copies, waits for them, and re-layouts  1.92 us (2%)
  between operations  1.3 us (2%)
    pallas_call x1, Pallas kernels, on_device(): pl.pallas_call(kernel, out_shape=jax.ShapeDtypeStruct((1, n, d), F32), in...  81 us
    unnamed x1, local copies, waits for them, and re-layouts  1.92 us

profile of v1, /device:TPU:2, one launch (start us, length us, event | category | flops | bytes accessed | tf_op | source)
XLA Modules:
  0.0 84.2 jit_solution(2391739073803886735)
XLA Ops:
  1.3 81.0 %towers.1 = f32[1,128,1152]{2,1,0:T(8,128)} custom-call(bf16[1,128,1152]{2,1,0:T(8,128)(2,1)} %pooled.1, f32[1,1152]{1,0:T(1,128)} %gain.1, bf16[1,1152,1152]{2,1,0:T(8,128)(2,1)} %weight.1, s32[128,128]{1,0:T(8,128)} %bitcast.5, f32[1,1]{1,0:T(1,128)} %bitcast.3.log_scale, f32[1,1]{1,0:T(1,128)} %bitcast.4.bias), custom_call_target="tpu_custom_call" | custom-call | tf_op jit(solution)/shard_map/towers/pallas_call | solution.py:452
  82.3 1.9 %copy.10 = f32[1,128,1152]{2,1,0:T(8,128)} copy(f32[1,128,1152]{2,1,0:T(8,128)} %towers.1) | data formatting | bytes 1179648

commit v2 on v1

v2 whole, which is shorter than its diff:
```python
import jax
import jax.numpy as jnp
from jax import lax
from jax.experimental import pallas as pl
from jax.experimental.pallas import tpu as pltpu
from jax.sharding import PartitionSpec as P

MESH = pl.DeviceIdType.MESH
BF = jnp.bfloat16
F32 = jnp.float32

Y_SLOT = {2: 0, 0: 1, 1: 2, -1: 3}
Z_SLOT = {4: 0, 3: 1, -3: 2, 2: 3, -2: 4, 1: 5, -1: 6, 0: 7}
UNITS = ((0, 384), (384, 256), (640, 384))
Z_OUT = tuple([(k, dist) for dist in (1, 2, 3) for k in range(4)] + [(k + 2 * d, 4) for k in (0, 1)] for d in (0, 1))
Z_BACK = ((0, 4), (1, 4)) + tuple((k, dist) for dist in (3, 2, 1) for k in (2, 3, 0, 1))


def kernel(
    pooled_hbm, gain_hbm, weight, ids_hbm, log_scale, bias, out,
    pooled, gain, ids, w_buf, emb, img, txt, coef, g_img, g_txt, s_img, s_x, s_txt, r_sib, r_z, r_y2, r_y1, r_x, r_fin,
    img_ids, txt_ids,
    in_sem, sx, rx, stx, rtx, sy, ry, sz, rz, ss, rs, ss2, rs2, szr, rzr, syr, ryr, sxr, rxr, sf, rf,
):
    t = lax.axis_index("tower")
    b = lax.axis_index("blk")
    c = lax.rem(b, 2)
    h = lax.rem(b // 2, 2)
    y = lax.rem(b // 4, 4)
    z = b // 16
    x = h * 2 + t
    is_img = t == 0
    is_txt = t == 1
    home = c == t
    guest = c != t

    def at(dx=0, dy=0, dz=0, dc=0):
        nx = lax.rem(x + dx + 4, 4)
        ny = lax.rem(y + dy + 4, 4)
        nz = lax.rem(z + dz + 8, 8)
        nc = lax.rem(c + dc, 2)
        return (lax.rem(nx, 2), ((nz * 4 + ny) * 2 + nx // 2) * 2 + nc)

    xp, xm, x2 = at(dx=1), at(dx=-1), at(dx=2)
    yd = (at(dy=1), at(dy=-1))
    zd = (at(dz=1), at(dz=-1))
    sib = at(dc=1)

    fetches = [
        pltpu.make_async_copy(a, b, in_sem.at[n])
        for n, (a, b) in enumerate(
            ((pooled_hbm.at[0], pooled), (gain_hbm, gain), (weight.at[0], w_buf), (ids_hbm, ids))
        )
    ]
    for fetch in fetches:
        fetch.start()

    barrier = pltpu.get_barrier_semaphore()
    for peer in (xp, xm, x2, yd[0], yd[1], zd[0], zd[1], sib):
        pl.semaphore_signal(barrier, 1, device_id=peer, device_id_type=MESH)

    def move(src, dst, send, recv, peer):
        return pltpu.make_async_remote_copy(
            src_ref=src, dst_ref=dst, send_sem=send, recv_sem=recv, device_id=peer, device_id_type=MESH
        )

    def rows(start, n=64):
        return pl.ds(start, n)

    def i_row(rel, q, half):
        return Y_SLOT[rel] * 256 + q * 128 + half * 64

    def t_row(rel, k):
        return Z_SLOT[rel] * 128 + k * 32

    fetches[0].wait()
    fetches[1].wait()
    values = pooled[...].astype(F32)
    center = values - jnp.mean(values, axis=-1, keepdims=True)
    spread = jnp.mean(center * center, axis=-1, keepdims=True)
    normed = (center * lax.rsqrt(spread + 1e-06) * gain[...]).astype(BF)
    fetches[2].wait()
    head = jnp.dot(normed, w_buf[...], preferred_element_type=F32)
    length = jnp.sum(head * head, axis=-1, keepdims=True)
    emb[...] = (head * lax.rsqrt(length + 1e-06)).astype(BF)
    pl.semaphore_wait(barrier, 8)

    def x_copies():
        res = []
        for half in (0, 1):
            for k, (peer, q) in enumerate(((xp, 0), (xm, 1), (x2, 1))):
                dst = img.at[rows(i_row(0, q, half))]
                res.append(move(emb.at[rows(half * 64)], dst, sx.at[k, half], rx.at[q, half], peer))
        return res

    def x_wait(q, half):
        dst = img.at[rows(i_row(0, q, half))]
        move(emb.at[rows(half * 64)], dst, sx.at[0, half], rx.at[q, half], xp).wait_recv()

    def tx_copy(k):
        return move(emb.at[rows(k * 32, 32)], txt.at[rows(t_row(0, k), 32)], stx.at[k], rtx.at[k], xm)

    def y_copy(d, q, half, dist):
        sign = 1 - 2 * d
        idx = q * 2 + half if dist == 1 else 4 + q
        src_rel = 0 if dist == 1 else -sign
        dst_rel = -sign if dist == 1 else 2
        return move(
            img.at[rows(i_row(src_rel, q, half))], img.at[rows(i_row(dst_rel, q, half))],
            sy.at[d, idx], ry.at[d, idx], yd[d],
        )

    def z_rel(d, dist):
        rel = -dist if d == 0 else dist
        return 4 if rel == -4 else rel

    def z_copy(d, i):
        k, dist = Z_OUT[d][i]
        src = txt.at[rows(t_row(z_rel(d, dist - 1), k), 32)]
        dst = txt.at[rows(t_row(z_rel(d, dist), k), 32)]
        return move(src, dst, sz.at[d, i], rz.at[d, i], zd[d])

    S_LIST = [(0, 0), (0, 1)] + [
        (z_rel(d, Z_OUT[d][i][1]), Z_OUT[d][i][0] // 2) for i in range(0, 14, 2) for d in (0, 1)
    ]

    def s_copy(n):
        rel, half = S_LIST[n]
        part = txt.at[rows(t_row(rel, half * 2))]
        return move(part, part, ss.at[n], rs.at[n], sib)

    @pl.when(is_img)
    def _():
        for copy in x_copies():
            copy.start()
        img[256:384, :] = emb[...]

    @pl.when(jnp.logical_and(is_txt, guest))
    def _():
        for k in range(4):
            tx_copy(k).start()

    @pl.when(jnp.logical_and(is_txt, home))
    def _():
        txt[896:1024, :] = emb[...]
        for k in range(4):
            for d in (0, 1):
                z_copy(d, k).start()
        for n in (0, 1):
            s_copy(n).start()

    def y_pair(q, half):
        for d in (0, 1):
            y_copy(d, q, half, 1).start()

    @pl.when(is_img)
    def _():
        y_pair(0, 0)
        y_pair(0, 1)

    fetches[3].wait()
    for rel, slot in Z_SLOT.items():
        row = ((lax.rem(z + rel + 8, 8) * 4 + y) * 2 + h) * 2 + t
        txt_ids[:, slot * 128 : slot * 128 + 128] = jnp.broadcast_to(ids[pl.ds(row, 1), :], (8, 128))
    for rel, slot in Y_SLOT.items():
        for q in (0, 1):
            row = ((z * 4 + lax.rem(y + rel + 4, 4)) * 2 + lax.rem(h + q, 2)) * 2 + c
            block = jnp.broadcast_to(ids[pl.ds(row, 1), :], (128, 128))
            start = slot * 256 + q * 128
            img_ids[start : start + 128, :] = block.T

    @pl.when(jnp.logical_and(is_img, home))
    def _():
        for k in range(4):
            tx_copy(k).wait_recv()
            for d in (0, 1):
                z_copy(d, k).start()
        for n in (0, 1):
            s_copy(n).start()

    def z_steps(*steps):
        @pl.when(home)
        def _():
            for i in steps:
                for d in (0, 1):
                    z_copy(d, i).wait_recv()
                    k, dist = Z_OUT[d][i]
                    if (k, dist + 1) in Z_OUT[d]:
                        z_copy(d, Z_OUT[d].index((k, dist + 1))).start()
                    if i % 2:
                        s_copy(2 + i // 2 * 2 + d).start()

    def y_relay(q):
        for d in (0, 1):
            y_copy(d, q, d, 1).wait_recv()
            y_copy(d, q, d, 2).start()

    z_steps(0, 1, 2, 3)

    @pl.when(is_img)
    def _():
        x_wait(1, 0)
        y_copy(0, 1, 0, 1).start()
        x_wait(1, 1)
        y_copy(1, 1, 1, 1).start()

    @pl.when(is_txt)
    def _():
        x_wait(0, 0)
        y_pair(0, 0)
        x_wait(1, 0)
        y_copy(0, 1, 0, 1).start()
        x_wait(0, 1)
        y_pair(0, 1)
        x_wait(1, 1)
        y_copy(1, 1, 1, 1).start()

    y_relay(0)
    z_steps(4, 5, 6, 7)
    y_relay(1)
    for d in (0, 1):
        y_copy(d, 1, 1 - d, 1).start()
    z_steps(*range(8, 14))

    @pl.when(guest)
    def _():
        for n in range(16):
            s_copy(n).wait_recv()

    scale = jnp.exp(jnp.full((1, 1), log_scale[0], F32))
    shift = bias[0]

    def tile(slot):
        part = pl.ds(slot * 256, 256)
        logits = scale * lax.dot_general(
            img[part, :], txt[...], (((1,), (1,)), ((), ())), preferred_element_type=F32
        ) + shift
        same = img_ids[part, 0:1] == txt_ids[0:1, :]
        weight_ = 1.0 / (1.0 + jnp.exp(jnp.minimum(jnp.where(same, logits, -logits), 88.0)))
        coef[part, :] = jnp.where(same, -weight_, weight_).astype(BF)
        g_img[part, :] = jnp.dot(coef[part, :], txt[...], preferred_element_type=F32)

    def yr_copy(d, q, half, dist):
        sign = 1 - 2 * d
        if dist == 2:
            return move(
                s_img.at[rows(i_row(2, q, half))], r_y2.at[rows((d * 2 + q) * 64)],
                syr.at[d, 4 + q], ryr.at[d, 4 + q], yd[d],
            )
        idx = q * 2 + half
        return move(
            s_img.at[rows(i_row(sign, q, half))], r_y1.at[rows((d * 4 + idx) * 64)],
            syr.at[d, idx], ryr.at[d, idx], yd[d],
        )

    tile(1)
    for d in (0, 1):
        for q in (0, 1):
            y_copy(d, q, d, 2).wait_recv()
    tile(0)
    s_img[0:256, :] = g_img[0:256, :].astype(BF)
    for q in (0, 1):
        for d in (0, 1):
            yr_copy(d, q, d, 2).start()
    for d in (0, 1):
        for q in (0, 1):
            y_copy(d, q, 1 - d, 1).wait_recv()
    tile(2)
    tile(3)

    def y_sums(d):
        sign = 1 - 2 * d
        for q in (0, 1):
            yr_copy(d, q, d, 2).wait_recv()
            for half in (0, 1):
                start = i_row(sign, q, half)
                total = g_img[start : start + 64, :]
                if half == d:
                    total = total + r_y2[(d * 2 + q) * 64 : (d * 2 + q) * 64 + 64, :].astype(F32)
                s_img[start : start + 64, :] = total.astype(BF)
                yr_copy(d, q, half, 1).start()

    def s2_copy(u):
        part = pl.ds(*UNITS[u])
        return move(s_txt.at[part], r_sib.at[part], ss2.at[u], rs2.at[u], sib)

    def text_dot(start, n):
        return lax.dot_general(
            coef[:, start : start + n], img[...], (((0,), (0,)), ((), ())), preferred_element_type=F32
        )

    def text_unit(u):
        start, n = UNITS[u]
        g_txt[start : start + n, :] = text_dot(start, n)

        @pl.when(guest)
        def _():
            s_txt[start : start + n, :] = g_txt[start : start + n, :].astype(BF)
            s2_copy(u).start()

    def back(d, i):
        k, dist = Z_BACK[i]
        rel = dist if d == 0 or dist == 4 else -dist
        return t_row(rel, k ^ (2 * d))

    def zr_copy(d, i):
        return move(
            s_txt.at[rows(back(d, i), 32)], r_z.at[rows((d * 14 + i) * 32, 32)], szr.at[d, i], rzr.at[d, i], zd[d]
        )

    def zr_take(d, i):
        zr_copy(d, i).wait_recv()
        return r_z[(d * 14 + i) * 32 : (d * 14 + i) * 32 + 32, :].astype(F32)

    def zr_steps(*steps):
        @pl.when(home)
        def _():
            for i in steps:
                for d in (0, 1):
                    start = back(d, i)
                    total = g_txt[start : start + 32, :] + r_sib[start : start + 32, :].astype(F32)
                    if i >= 4:
                        total = total + zr_take(d, i - 4)
                    s_txt[start : start + 32, :] = total.astype(BF)
                    zr_copy(d, i).start()

    def xr_copies(q, half):
        src = s_x.at[rows(q * 128 + half * 64)]
        if q == 0:
            return [(is_txt, move(src, r_x.at[rows(half * 64)], sxr.at[q, half], rxr.at[0, half], xm))]
        return [
            (is_txt, move(src, r_x.at[rows(128 + half * 64)], sxr.at[q, half], rxr.at[1, half], xp)),
            (is_img, move(src, r_x.at[rows(256 + half * 64)], sxr.at[q, half], rxr.at[2, half], x2)),
        ]

    def y_final(q, half):
        for d in (0, 1):
            yr_copy(d, q, half, 1).wait_recv()
        start = i_row(0, q, half)
        k = (q * 2 + half) * 64
        total = g_img[start : start + 64, :] + r_y1[k : k + 64, :].astype(F32) + r_y1[256 + k : 256 + k + 64, :].astype(F32)
        if q == 0:
            g_img[start : start + 64, :] = total
        s_x[q * 128 + half * 64 : q * 128 + half * 64 + 64, :] = total.astype(BF)
        for cond, copy in xr_copies(q, half):
            pl.when(cond)(copy.start)

    def s2_wait(*units):
        @pl.when(home)
        def _():
            for u in units:
                s2_copy(u).wait_recv()

    text_unit(0)
    y_sums(0)
    y_sums(1)
    s2_wait(0)
    zr_steps(0, 1, 2, 3)
    text_unit(1)
    text_unit(2)
    s2_wait(1, 2)
    zr_steps(4, 5, 6, 7)
    y_final(0, 0)
    y_final(0, 1)
    zr_steps(8, 9)
    y_final(1, 0)
    zr_steps(10, 11)
    y_final(1, 1)
    zr_steps(12, 13)

    def f_copy(k):
        return move(s_txt.at[rows(t_row(0, k), 32)], r_fin.at[rows(k * 32, 32)], sf.at[k], rf.at[k], xp)

    @pl.when(home)
    def _():
        for k in (2, 3, 0, 1):
            start = t_row(0, k)
            total = g_txt[start : start + 32, :] + r_sib[start : start + 32, :].astype(F32)
            for d in (0, 1):
                total = total + zr_take(d, 10 + ((2, 3, 0, 1).index(k ^ (2 * d))))

            @pl.when(is_txt)
            def _():
                out[0, k * 32 : k * 32 + 32, :] = total

            @pl.when(is_img)
            def _():
                s_txt[start : start + 32, :] = total.astype(BF)
                f_copy(k).start()

    @pl.when(is_img)
    def _():
        for half in (0, 1):
            for k in range(3):
                part = r_x.at[rows(k * 128 + half * 64)]
                move(part, part, sxr.at[0, half], rxr.at[k, half], xp).wait_recv()
            total = g_img[i_row(0, 0, half) : i_row(0, 0, half) + 64, :]
            for k in range(3):
                total = total + r_x[k * 128 + half * 64 : k * 128 + half * 64 + 64, :].astype(F32)
            out[0, half * 64 : half * 64 + 64, :] = total

    @pl.when(jnp.logical_and(is_txt, guest))
    def _():
        for k in (2, 3, 0, 1):
            f_copy(k).wait_recv()
            out[0, k * 32 : k * 32 + 32, :] = r_fin[k * 32 : k * 32 + 32, :].astype(F32)

    @pl.when(is_img)
    def _():
        for copy in x_copies():
            copy.wait_send()

    @pl.when(jnp.logical_and(is_txt, guest))
    def _():
        for k in range(4):
            tx_copy(k).wait_send()

    for d in (0, 1):
        for q in (0, 1):
            for half in (0, 1):
                y_copy(d, q, half, 1).wait_send()
                yr_copy(d, q, half, 1).wait_send()
            y_copy(d, q, d, 2).wait_send()
            yr_copy(d, q, d, 2).wait_send()

    @pl.when(home)
    def _():
        for i in range(14):
            for d in (0, 1):
                z_copy(d, i).wait_send()
                zr_copy(d, i).wait_send()
        for n in range(16):
            s_copy(n).wait_send()

    @pl.when(guest)
    def _():
        for u in range(3):
            s2_copy(u).wait_send()

    for q in (0, 1):
        for half in (0, 1):
            for cond, copy in xr_copies(q, half):
                pl.when(cond)(copy.wait_send)

    @pl.when(jnp.logical_and(is_img, home))
    def _():
        for k in range(4):
            f_copy(k).wait_send()


def on_device(pooled, final_gain, head_weight, pair_ids, log_scale, bias):
    n, d = pooled.shape[1:]
    hbm = pl.BlockSpec(memory_space=pl.ANY)
    smem = pl.BlockSpec(memory_space=pltpu.SMEM)
    buf = lambda r, kind=BF: pltpu.VMEM((r, d), kind)
    dma = pltpu.SemaphoreType.DMA
    return pl.pallas_call(
        kernel,
        out_shape=jax.ShapeDtypeStruct((1, n, d), F32),
        in_specs=[hbm, hbm, hbm, hbm, smem, smem],
        out_specs=pl.BlockSpec(memory_space=pltpu.VMEM),
        scratch_shapes=[
            buf(n), buf(1, F32), pltpu.VMEM((128, 128), jnp.int32), buf(d), buf(128), buf(1024), buf(1024), pltpu.VMEM((1024, 1024), BF), buf(1024, F32), buf(1024, F32),
            buf(1024), buf(256), buf(1024), buf(1024), buf(14 * 64), buf(4 * 64), buf(8 * 64), buf(6 * 64), buf(128),
            pltpu.VMEM((1024, 128), jnp.int32), pltpu.VMEM((8, 1024), jnp.int32),
            dma((4,)), dma((3, 2)), dma((2, 2)), dma((4,)), dma((4,)), dma((2, 6)), dma((2, 6)), dma((2, 14)), dma((2, 14)),
            dma((16,)), dma((16,)), dma((3,)), dma((3,)), dma((2, 14)), dma((2, 14)), dma((2, 6)), dma((2, 6)),
            dma((2, 2)), dma((3, 2)), dma((4,)), dma((4,)),
        ],
        compiler_params=pltpu.CompilerParams(collective_id=0, has_side_effects=True, vmem_limit_bytes=60 * 2**20),
        name="towers",
    )(pooled, final_gain, head_weight, pair_ids.reshape(128, 128), log_scale, bias)


def solution(mesh):
    placed = (P("tower", "blk", None), P("tower", None), P("tower", None, None), P(), P(), P())
    return jax.shard_map(
        on_device, mesh=mesh, in_specs=placed, out_specs=P("tower", "blk", None), check_vma=False
    )
```

time: 84.4 us -> 76.4 us (0.905)
  Pallas kernels: 81 us -> 73 us
    pallas_call x1, Pallas kernels: 81 us -> 73 us  [on_device(): pl.pallas_call(kernel, out_shape=jax.ShapeDtypeStruct((1, n, d), F32), in...]
where the time goes in v2:
time: 76.4 us; the launch traced here: 76.2 us
  Pallas kernels  73 us (96%)
  local copies, waits for them, and re-layouts  1.92 us (3%)
  between operations  1.3 us (2%)
    pallas_call x1, Pallas kernels, on_device(): pl.pallas_call(kernel, out_shape=jax.ShapeDtypeStruct((1, n, d), F32), in...  73 us
    unnamed x1, local copies, waits for them, and re-layouts  1.92 us

profile of v2, /device:TPU:2, one launch (start us, length us, event | category | flops | bytes accessed | tf_op | source)
XLA Modules:
  0.0 76.2 jit_solution(2519079404382744102)
XLA Ops:
  1.3 73.0 %towers.1 = f32[1,128,1152]{2,1,0:T(8,128)} custom-call(bf16[1,128,1152]{2,1,0:T(8,128)(2,1)} %pooled_hbm.1, f32[1,1152]{1,0:T(1,128)} %gain_hbm.1, bf16[1,1152,1152]{2,1,0:T(8,128)(2,1)} %weight.1, s32[128,128]{1,0:T(8,128)} %bitcast.1, f32[1]{0:T(128)S(6)} %copy.8.log_scale, f32[1]{0:T(128)S(6)} %copy.9.bias), custom_call_target="tpu_custom_call" | custom-call | tf_op jit(solution)/shard_map/towers/pallas_call | solution.py:457
  74.3 1.9 %copy.10 = f32[1,128,1152]{2,1,0:T(8,128)} copy(f32[1,128,1152]{2,1,0:T(8,128)} %towers.1) | data formatting | bytes 1179648

commit v3 on v2

--- a/solution.py
+++ b/solution.py
@@ -9,7 +9,7 @@
 BF = jnp.bfloat16
 F32 = jnp.float32
 
-Y_SLOT = {2: 0, 0: 1, 1: 2, -1: 3}
+I_SLOT = {(2, 0): 0, (2, 1): 1, (0, 0): 2, (0, 1): 3, (1, 0): 4, (-1, 0): 5, (1, 1): 6, (-1, 1): 7}
 Z_SLOT = {4: 0, 3: 1, -3: 2, 2: 3, -2: 4, 1: 5, -1: 6, 0: 7}
 UNITS = ((0, 384), (384, 256), (640, 384))
 Z_OUT = tuple([(k, dist) for dist in (1, 2, 3) for k in range(4)] + [(k + 2 * d, 4) for k in (0, 1)] for d in (0, 1))
@@ -20,7 +20,7 @@
     pooled_hbm, gain_hbm, weight, ids_hbm, log_scale, bias, out,
     pooled, gain, ids, w_buf, emb, img, txt, coef, g_img, g_txt, s_img, s_x, s_txt, r_sib, r_z, r_y2, r_y1, r_x, r_fin,
     img_ids, txt_ids,
-    in_sem, sx, rx, stx, rtx, sy, ry, sz, rz, ss, rs, ss2, rs2, szr, rzr, syr, ryr, sxr, rxr, sf, rf,
+    in_sem, sx, rx, sxw, rxw, stx, rtx, sy, ry, sz, rz, ss, rs, ss2, rs2, szr, rzr, syr, ryr, sxr, rxr, sf, rf,
 ):
     t = lax.axis_index("tower")
     b = lax.axis_index("blk")
@@ -68,7 +68,7 @@
         return pl.ds(start, n)
 
     def i_row(rel, q, half):
-        return Y_SLOT[rel] * 256 + q * 128 + half * 64
+        return I_SLOT[rel, q] * 128 + half * 64
 
     def t_row(rel, k):
         return Z_SLOT[rel] * 128 + k * 32
@@ -162,12 +162,10 @@
     for rel, slot in Z_SLOT.items():
         row = ((lax.rem(z + rel + 8, 8) * 4 + y) * 2 + h) * 2 + t
         txt_ids[:, slot * 128 : slot * 128 + 128] = jnp.broadcast_to(ids[pl.ds(row, 1), :], (8, 128))
-    for rel, slot in Y_SLOT.items():
-        for q in (0, 1):
-            row = ((z * 4 + lax.rem(y + rel + 4, 4)) * 2 + lax.rem(h + q, 2)) * 2 + c
-            block = jnp.broadcast_to(ids[pl.ds(row, 1), :], (128, 128))
-            start = slot * 256 + q * 128
-            img_ids[start : start + 128, :] = block.T
+    for (rel, q), slot in I_SLOT.items():
+        row = ((z * 4 + lax.rem(y + rel + 4, 4)) * 2 + lax.rem(h + q, 2)) * 2 + c
+        block = jnp.broadcast_to(ids[pl.ds(row, 1), :], (128, 128))
+        img_ids[slot * 128 : slot * 128 + 128, :] = block.T
 
     @pl.when(jnp.logical_and(is_img, home))
     def _():
@@ -195,32 +193,61 @@
             y_copy(d, q, d, 1).wait_recv()
             y_copy(d, q, d, 2).start()
 
-    z_steps(0, 1, 2, 3)
+    def xw_copy(q, half):
+        return move(
+            img.at[rows(i_row(2, 0, half))], img.at[rows(i_row(2, q, half))], sxw.at[q, half], rxw.at[q, half],
+            (xp, xm)[q],
+        )
 
     @pl.when(is_img)
     def _():
+        y_relay(0)
+        z_steps(0, 1, 2, 3)
         x_wait(1, 0)
         y_copy(0, 1, 0, 1).start()
         x_wait(1, 1)
         y_copy(1, 1, 1, 1).start()
+        for d in (0, 1):
+            y_copy(d, 0, d, 2).wait_recv()
+            for q in (0, 1):
+                xw_copy(q, d).start()
+        z_steps(4, 5, 6, 7)
+        y_relay(1)
+        for d in (0, 1):
+            y_copy(d, 1, 1 - d, 1).start()
 
     @pl.when(is_txt)
     def _():
-        x_wait(0, 0)
-        y_pair(0, 0)
-        x_wait(1, 0)
-        y_copy(0, 1, 0, 1).start()
-        x_wait(0, 1)
-        y_pair(0, 1)
-        x_wait(1, 1)
-        y_copy(1, 1, 1, 1).start()
-
-    y_relay(0)
-    z_steps(4, 5, 6, 7)
-    y_relay(1)
-    for d in (0, 1):
-        y_copy(d, 1, 1 - d, 1).start()
+        z_steps(0, 1, 2, 3)
+        for q in (0, 1):
+            x_wait(q, 0)
+            y_pair(q, 0)
+        z_steps(4, 5, 6, 7)
+        for q in (0, 1):
+            x_wait(q, 1)
+            y_pair(q, 1)
+
     z_steps(*range(8, 14))
+
+    def y_need(q):
+        for d in (0, 1):
+            y_copy(d, q, 1 - d, 1).wait_recv()
+
+            @pl.when(is_txt)
+            def _():
+                y_copy(d, q, d, 1).wait_recv()
+
+    def far_need():
+        @pl.when(is_img)
+        def _():
+            for d in (0, 1):
+                y_copy(d, 1, d, 2).wait_recv()
+
+        @pl.when(is_txt)
+        def _():
+            for q in (0, 1):
+                for half in (0, 1):
+                    xw_copy(q, half).wait_recv()
 
     @pl.when(guest)
     def _():
@@ -253,32 +280,31 @@
             syr.at[d, idx], ryr.at[d, idx], yd[d],
         )
 
-    tile(1)
-    for d in (0, 1):
-        for q in (0, 1):
-            y_copy(d, q, d, 2).wait_recv()
+    def y_send(q, merged):
+        for d in (0, 1):
+            sign = 1 - 2 * d
+            half = d if merged else 1 - d
+            start = i_row(sign, q, half)
+            total = g_img[start : start + 64, :]
+            if merged:
+                yr_copy(d, q, d, 2).wait_recv()
+                total = total + r_y2[(d * 2 + q) * 64 : (d * 2 + q) * 64 + 64, :].astype(F32)
+            s_img[start : start + 64, :] = total.astype(BF)
+            yr_copy(d, q, half, 1).start()
+
+    y_need(0)
+    tile(2)
+    y_send(0, False)
+    far_need()
     tile(0)
     s_img[0:256, :] = g_img[0:256, :].astype(BF)
     for q in (0, 1):
         for d in (0, 1):
             yr_copy(d, q, d, 2).start()
-    for d in (0, 1):
-        for q in (0, 1):
-            y_copy(d, q, 1 - d, 1).wait_recv()
-    tile(2)
+    y_need(1)
     tile(3)
-
-    def y_sums(d):
-        sign = 1 - 2 * d
-        for q in (0, 1):
-            yr_copy(d, q, d, 2).wait_recv()
-            for half in (0, 1):
-                start = i_row(sign, q, half)
-                total = g_img[start : start + 64, :]
-                if half == d:
-                    total = total + r_y2[(d * 2 + q) * 64 : (d * 2 + q) * 64 + 64, :].astype(F32)
-                s_img[start : start + 64, :] = total.astype(BF)
-                yr_copy(d, q, half, 1).start()
+    y_send(1, False)
+    tile(1)
 
     def s2_copy(u):
         part = pl.ds(*UNITS[u])
@@ -352,8 +378,8 @@
                 s2_copy(u).wait_recv()
 
     text_unit(0)
-    y_sums(0)
-    y_sums(1)
+    y_send(0, True)
+    y_send(1, True)
     s2_wait(0)
     zr_steps(0, 1, 2, 3)
     text_unit(1)
@@ -409,6 +435,10 @@
     def _():
         for copy in x_copies():
             copy.wait_send()
+        for q in (0, 1):
+            for d in (0, 1):
+                y_copy(d, q, d, 2).wait_send()
+                xw_copy(q, d).wait_send()
 
     @pl.when(jnp.logical_and(is_txt, guest))
     def _():
@@ -420,7 +450,6 @@
             for half in (0, 1):
                 y_copy(d, q, half, 1).wait_send()
                 yr_copy(d, q, half, 1).wait_send()
-            y_copy(d, q, d, 2).wait_send()
             yr_copy(d, q, d, 2).wait_send()
 
     @pl.when(home)
@@ -463,7 +492,7 @@
             buf(n), buf(1, F32), pltpu.VMEM((128, 128), jnp.int32), buf(d), buf(128), buf(1024), buf(1024), pltpu.VMEM((1024, 1024), BF), buf(1024, F32), buf(1024, F32),
             buf(1024), buf(256), buf(1024), buf(1024), buf(14 * 64), buf(4 * 64), buf(8 * 64), buf(6 * 64), buf(128),
             pltpu.VMEM((1024, 128), jnp.int32), pltpu.VMEM((8, 1024), jnp.int32),
-            dma((4,)), dma((3, 2)), dma((2, 2)), dma((4,)), dma((4,)), dma((2, 6)), dma((2, 6)), dma((2, 14)), dma((2, 14)),
+            dma((4,)), dma((3, 2)), dma((2, 2)), dma((2, 2)), dma((2, 2)), dma((4,)), dma((4,)), dma((2, 6)), dma((2, 6)), dma((2, 14)), dma((2, 14)),
             dma((16,)), dma((16,)), dma((3,)), dma((3,)), dma((2, 14)), dma((2, 14)), dma((2, 6)), dma((2, 6)),
             dma((2, 2)), dma((3, 2)), dma((4,)), dma((4,)),
         ],

time: 76.4 us -> 77.3 us (1.012)
  Pallas kernels: 73 us -> 73.9 us
    pallas_call x1, Pallas kernels: 73 us -> 73.9 us  [on_device(): pl.pallas_call(kernel, out_shape=jax.ShapeDtypeStruct((1, n, d), F32), in...]
where the time goes in v3:
time: 77.3 us; the launch traced here: 77.1 us
  Pallas kernels  73.9 us (96%)
  local copies, waits for them, and re-layouts  1.92 us (2%)
  between operations  1.3 us (2%)
    pallas_call x1, Pallas kernels, on_device(): pl.pallas_call(kernel, out_shape=jax.ShapeDtypeStruct((1, n, d), F32), in...  73.9 us
    unnamed x1, local copies, waits for them, and re-layouts  1.92 us

profile of v3, /device:TPU:2, one launch (start us, length us, event | category | flops | bytes accessed | tf_op | source)
XLA Modules:
  0.0 77.1 jit_solution(6527293551830165499)
XLA Ops:
  1.3 73.9 %towers.1 = f32[1,128,1152]{2,1,0:T(8,128)} custom-call(bf16[1,128,1152]{2,1,0:T(8,128)(2,1)} %pooled_hbm.1, f32[1,1152]{1,0:T(1,128)} %gain_hbm.1, bf16[1,1152,1152]{2,1,0:T(8,128)(2,1)} %weight.1, s32[128,128]{1,0:T(8,128)} %bitcast.1, f32[1]{0:T(128)S(6)} %copy.8.log_scale, f32[1]{0:T(128)S(6)} %copy.9.bias), custom_call_target="tpu_custom_call" | custom-call | tf_op jit(solution)/shard_map/towers/pallas_call | solution.py:486
  75.2 1.9 %copy.10 = f32[1,128,1152]{2,1,0:T(8,128)} copy(f32[1,128,1152]{2,1,0:T(8,128)} %towers.1) | data formatting | bytes 1179648

commit v4 on v3

--- a/solution.py
+++ b/solution.py
@@ -88,7 +88,7 @@
     def x_copies():
         res = []
         for half in (0, 1):
-            for k, (peer, q) in enumerate(((xp, 0), (xm, 1), (x2, 1))):
+            for k, (peer, q) in enumerate(((x2, 1), (xp, 0), (xm, 1))):
                 dst = img.at[rows(i_row(0, q, half))]
                 res.append(move(emb.at[rows(half * 64)], dst, sx.at[k, half], rx.at[q, half], peer))
         return res
@@ -202,19 +202,20 @@
     @pl.when(is_img)
     def _():
         y_relay(0)
-        z_steps(0, 1, 2, 3)
         x_wait(1, 0)
         y_copy(0, 1, 0, 1).start()
+        z_steps(0, 1, 2, 3)
         x_wait(1, 1)
         y_copy(1, 1, 1, 1).start()
+        z_steps(4, 5, 6, 7)
         for d in (0, 1):
             y_copy(d, 0, d, 2).wait_recv()
             for q in (0, 1):
                 xw_copy(q, d).start()
-        z_steps(4, 5, 6, 7)
         y_relay(1)
         for d in (0, 1):
             y_copy(d, 1, 1 - d, 1).start()
+        z_steps(8, 9)
 
     @pl.when(is_txt)
     def _():
@@ -222,12 +223,18 @@
         for q in (0, 1):
             x_wait(q, 0)
             y_pair(q, 0)
-        z_steps(4, 5, 6, 7)
+        z_steps(4, 5, 6, 7, 8, 9)
         for q in (0, 1):
             x_wait(q, 1)
             y_pair(q, 1)
 
-    z_steps(*range(8, 14))
+    z_steps(10, 11)
+
+    def guest_need(*numbers):
+        @pl.when(guest)
+        def _():
+            for n in numbers:
+                s_copy(n).wait_recv()
 
     def y_need(q):
         for d in (0, 1):
@@ -249,23 +256,23 @@
                 for half in (0, 1):
                     xw_copy(q, half).wait_recv()
 
-    @pl.when(guest)
-    def _():
-        for n in range(16):
-            s_copy(n).wait_recv()
-
     scale = jnp.exp(jnp.full((1, 1), log_scale[0], F32))
     shift = bias[0]
 
-    def tile(slot):
+    def tile(slot, start=0, n=1024):
         part = pl.ds(slot * 256, 256)
+        cols = pl.ds(start, n)
         logits = scale * lax.dot_general(
-            img[part, :], txt[...], (((1,), (1,)), ((), ())), preferred_element_type=F32
+            img[part, :], txt[cols, :], (((1,), (1,)), ((), ())), preferred_element_type=F32
         ) + shift
-        same = img_ids[part, 0:1] == txt_ids[0:1, :]
+        same = img_ids[part, 0:1] == txt_ids[0:1, cols]
         weight_ = 1.0 / (1.0 + jnp.exp(jnp.minimum(jnp.where(same, logits, -logits), 88.0)))
-        coef[part, :] = jnp.where(same, -weight_, weight_).astype(BF)
-        g_img[part, :] = jnp.dot(coef[part, :], txt[...], preferred_element_type=F32)
+        coef[part, cols] = jnp.where(same, -weight_, weight_).astype(BF)
+        total = jnp.dot(coef[part, cols], txt[cols, :], preferred_element_type=F32)
+        if start + n < 1024 or n == 1024:
+            g_img[part, :] = total + g_img[part, :] if n < 1024 else total
+        else:
+            g_img[part, :] = total
 
     def yr_copy(d, q, half, dist):
         sign = 1 - 2 * d
@@ -292,8 +299,13 @@
             s_img[start : start + 64, :] = total.astype(BF)
             yr_copy(d, q, half, 1).start()
 
+    guest_need(*range(11), 12)
     y_need(0)
-    tile(2)
+    tile(2, 256, 768)
+    tile(1, 256, 768)
+    z_steps(12, 13)
+    guest_need(11, 13, 14, 15)
+    tile(2, 0, 256)
     y_send(0, False)
     far_need()
     tile(0)
@@ -304,7 +316,7 @@
     y_need(1)
     tile(3)
     y_send(1, False)
-    tile(1)
+    tile(1, 0, 256)
 
     def s2_copy(u):
         part = pl.ds(*UNITS[u])
@@ -378,21 +390,19 @@
                 s2_copy(u).wait_recv()
 
     text_unit(0)
-    y_send(0, True)
-    y_send(1, True)
     s2_wait(0)
     zr_steps(0, 1, 2, 3)
+    y_send(0, True)
     text_unit(1)
     text_unit(2)
+    y_send(1, True)
     s2_wait(1, 2)
-    zr_steps(4, 5, 6, 7)
+    zr_steps(*range(4, 12))
     y_final(0, 0)
     y_final(0, 1)
-    zr_steps(8, 9)
+    zr_steps(12, 13)
     y_final(1, 0)
-    zr_steps(10, 11)
     y_final(1, 1)
-    zr_steps(12, 13)
 
     def f_copy(k):
         return move(s_txt.at[rows(t_row(0, k), 32)], r_fin.at[rows(k * 32, 32)], sf.at[k], rf.at[k], xp)
@@ -485,7 +495,7 @@
     dma = pltpu.SemaphoreType.DMA
     return pl.pallas_call(
         kernel,
-        out_shape=jax.ShapeDtypeStruct((1, n, d), F32),
+        out_shape=pltpu.VMEM((1, n, d), F32),
         in_specs=[hbm, hbm, hbm, hbm, smem, smem],
         out_specs=pl.BlockSpec(memory_space=pltpu.VMEM),
         scratch_shapes=[
@@ -496,7 +506,7 @@
             dma((16,)), dma((16,)), dma((3,)), dma((3,)), dma((2, 14)), dma((2, 14)), dma((2, 6)), dma((2, 6)),
             dma((2, 2)), dma((3, 2)), dma((4,)), dma((4,)),
         ],
-        compiler_params=pltpu.CompilerParams(collective_id=0, has_side_effects=True, vmem_limit_bytes=60 * 2**20),
+        compiler_params=pltpu.CompilerParams(collective_id=0, has_side_effects=True, vmem_limit_bytes=67043328 - 600000),
         name="towers",
     )(pooled, final_gain, head_weight, pair_ids.reshape(128, 128), log_scale, bias)
 

time: 77.3 us -> 71.5 us (0.925); the launches traced: 77.1 us -> 70.1 us
  Pallas kernels: 73.9 us -> 68 us
  local copies, waits for them, and re-layouts: 1.92 us -> 0.82 us
    pallas_call x1, Pallas kernels: 73.9 us -> 68 us  [on_device(): pl.pallas_call(kernel, out_shape=pltpu.VMEM((1, n, d), F32), in_specs=[hb...]
    unnamed x1, local copies, waits for them, and re-layouts: 1.92 us -> 0.82 us
where the time goes in v4:
time: 71.5 us; the launch traced here: 70.1 us
  Pallas kernels  68 us (95%)
  between operations  1.3 us (2%)
  local copies, waits for them, and re-layouts  0.82 us (1%)
    pallas_call x1, Pallas kernels, on_device(): pl.pallas_call(kernel, out_shape=pltpu.VMEM((1, n, d), F32), in_specs=[hb...  68 us

profile of v4, /device:TPU:2, one launch (start us, length us, event | category | flops | bytes accessed | tf_op | source)
XLA Modules:
  0.0 70.1 jit_solution(4094381800823141426)
XLA Ops:
  1.3 68.0 %towers.1 = f32[1,128,1152]{2,1,0:T(8,128)S(1)} custom-call(bf16[1,128,1152]{2,1,0:T(8,128)(2,1)} %pooled_hbm.1, f32[1,1152]{1,0:T(1,128)} %gain_hbm.1, bf16[1,1152,1152]{2,1,0:T(8,128)(2,1)} %weight.1, s32[128,128]{1,0:T(8,128)} %bitcast.1, f32[1]{0:T(128)S(6)} %copy.9.log_scale, f32[1]{0:T(128)S(6)} %copy.10.bias), custom_call_target="tpu_custom_call" | custom-call | tf_op jit(solution)/shard_map/towers/pallas_call | solution.py:496
  69.3 0.8 %copy.8 = f32[1,128,1152]{2,1,0:T(8,128)} copy(f32[1,128,1152]{2,1,0:T(8,128)S(1)} %towers.1) | data formatting | bytes 1179648

commit v5 on v4

--- a/solution.py
+++ b/solution.py
@@ -274,30 +274,36 @@
         else:
             g_img[part, :] = total
 
-    def yr_copy(d, q, half, dist):
+    def q_row(rel, q, k):
+        return I_SLOT[rel, q] * 128 + k * 32
+
+    def yr_copy(d, q, k, dist):
         sign = 1 - 2 * d
         if dist == 2:
+            n = q * 2 + k - 2 * d
             return move(
-                s_img.at[rows(i_row(2, q, half))], r_y2.at[rows((d * 2 + q) * 64)],
-                syr.at[d, 4 + q], ryr.at[d, 4 + q], yd[d],
+                s_img.at[rows(q_row(2, q, k), 32)], r_y2.at[rows((d * 4 + n) * 32, 32)],
+                syr.at[d, 8 + n], ryr.at[d, 8 + n], yd[d],
             )
-        idx = q * 2 + half
+        n = q * 4 + k
         return move(
-            s_img.at[rows(i_row(sign, q, half))], r_y1.at[rows((d * 4 + idx) * 64)],
-            syr.at[d, idx], ryr.at[d, idx], yd[d],
+            s_img.at[rows(q_row(sign, q, k), 32)], r_y1.at[rows((d * 8 + n) * 32, 32)],
+            syr.at[d, n], ryr.at[d, n], yd[d],
         )
 
     def y_send(q, merged):
-        for d in (0, 1):
-            sign = 1 - 2 * d
-            half = d if merged else 1 - d
-            start = i_row(sign, q, half)
-            total = g_img[start : start + 64, :]
-            if merged:
-                yr_copy(d, q, d, 2).wait_recv()
-                total = total + r_y2[(d * 2 + q) * 64 : (d * 2 + q) * 64 + 64, :].astype(F32)
-            s_img[start : start + 64, :] = total.astype(BF)
-            yr_copy(d, q, half, 1).start()
+        for j in (0, 1):
+            for d in (0, 1):
+                sign = 1 - 2 * d
+                k = 2 * (d if merged else 1 - d) + j
+                start = q_row(sign, q, k)
+                total = g_img[start : start + 32, :]
+                if merged:
+                    yr_copy(d, q, k, 2).wait_recv()
+                    far = (d * 4 + q * 2 + j) * 32
+                    total = total + r_y2[far : far + 32, :].astype(F32)
+                s_img[start : start + 32, :] = total.astype(BF)
+                yr_copy(d, q, k, 1).start()
 
     guest_need(*range(11), 12)
     y_need(0)
@@ -311,8 +317,9 @@
     tile(0)
     s_img[0:256, :] = g_img[0:256, :].astype(BF)
     for q in (0, 1):
-        for d in (0, 1):
-            yr_copy(d, q, d, 2).start()
+        for j in (0, 1):
+            for d in (0, 1):
+                yr_copy(d, q, 2 * d + j, 2).start()
     y_need(1)
     tile(3)
     y_send(1, False)
@@ -362,26 +369,29 @@
                     s_txt[start : start + 32, :] = total.astype(BF)
                     zr_copy(d, i).start()
 
-    def xr_copies(q, half):
-        src = s_x.at[rows(q * 128 + half * 64)]
+    def xr_copies(q, k):
+        src = s_x.at[rows(q * 128 + k * 32, 32)]
         if q == 0:
-            return [(is_txt, move(src, r_x.at[rows(half * 64)], sxr.at[q, half], rxr.at[0, half], xm))]
+            return [(is_txt, move(src, r_x.at[rows(k * 32, 32)], sxr.at[q, k], rxr.at[0, k], xm))]
         return [
-            (is_txt, move(src, r_x.at[rows(128 + half * 64)], sxr.at[q, half], rxr.at[1, half], xp)),
-            (is_img, move(src, r_x.at[rows(256 + half * 64)], sxr.at[q, half], rxr.at[2, half], x2)),
+            (is_txt, move(src, r_x.at[rows(128 + k * 32, 32)], sxr.at[q, k], rxr.at[1, k], xp)),
+            (is_img, move(src, r_x.at[rows(256 + k * 32, 32)], sxr.at[q, k], rxr.at[2, k], x2)),
         ]
 
-    def y_final(q, half):
-        for d in (0, 1):
-            yr_copy(d, q, half, 1).wait_recv()
-        start = i_row(0, q, half)
-        k = (q * 2 + half) * 64
-        total = g_img[start : start + 64, :] + r_y1[k : k + 64, :].astype(F32) + r_y1[256 + k : 256 + k + 64, :].astype(F32)
-        if q == 0:
-            g_img[start : start + 64, :] = total
-        s_x[q * 128 + half * 64 : q * 128 + half * 64 + 64, :] = total.astype(BF)
-        for cond, copy in xr_copies(q, half):
-            pl.when(cond)(copy.start)
+    LAST = (0, 2, 1, 3)
+
+    def y_final(q):
+        for k in LAST:
+            for d in (0, 1):
+                yr_copy(d, q, k, 1).wait_recv()
+            start = q_row(0, q, k)
+            n = (q * 4 + k) * 32
+            total = g_img[start : start + 32, :] + r_y1[n : n + 32, :].astype(F32) + r_y1[256 + n : 288 + n, :].astype(F32)
+            if q == 0:
+                g_img[start : start + 32, :] = total
+            s_x[q * 128 + k * 32 : q * 128 + k * 32 + 32, :] = total.astype(BF)
+            for cond, copy in xr_copies(q, k):
+                pl.when(cond)(copy.start)
 
     def s2_wait(*units):
         @pl.when(home)
@@ -390,19 +400,28 @@
                 s2_copy(u).wait_recv()
 
     text_unit(0)
+    y_send(0, True)
     s2_wait(0)
     zr_steps(0, 1, 2, 3)
-    y_send(0, True)
     text_unit(1)
     text_unit(2)
     y_send(1, True)
     s2_wait(1, 2)
-    zr_steps(*range(4, 12))
-    y_final(0, 0)
-    y_final(0, 1)
-    zr_steps(12, 13)
-    y_final(1, 0)
-    y_final(1, 1)
+    zr_steps(*range(4, 8))
+
+    @pl.when(is_txt)
+    def _():
+        y_final(0)
+        zr_steps(8, 9, 10, 11)
+        y_final(1)
+        zr_steps(12, 13)
+
+    @pl.when(is_img)
+    def _():
+        zr_steps(8, 9, 10, 11)
+        y_final(0)
+        zr_steps(12, 13)
+        y_final(1)
 
     def f_copy(k):
         return move(s_txt.at[rows(t_row(0, k), 32)], r_fin.at[rows(k * 32, 32)], sf.at[k], rf.at[k], xp)
@@ -426,14 +445,14 @@
 
     @pl.when(is_img)
     def _():
-        for half in (0, 1):
-            for k in range(3):
-                part = r_x.at[rows(k * 128 + half * 64)]
-                move(part, part, sxr.at[0, half], rxr.at[k, half], xp).wait_recv()
-            total = g_img[i_row(0, 0, half) : i_row(0, 0, half) + 64, :]
-            for k in range(3):
-                total = total + r_x[k * 128 + half * 64 : k * 128 + half * 64 + 64, :].astype(F32)
-            out[0, half * 64 : half * 64 + 64, :] = total
+        for k in LAST:
+            start = q_row(0, 0, k)
+            total = g_img[start : start + 32, :]
+            for n in range(3):
+                part = rows(n * 128 + k * 32, 32)
+                move(r_x.at[part], r_x.at[part], sxr.at[0, k], rxr.at[n, k], xp).wait_recv()
+                total = total + r_x[part, :].astype(F32)
+            out[0, k * 32 : k * 32 + 32, :] = total
 
     @pl.when(jnp.logical_and(is_txt, guest))
     def _():
@@ -459,8 +478,9 @@
         for q in (0, 1):
             for half in (0, 1):
                 y_copy(d, q, half, 1).wait_send()
-                yr_copy(d, q, half, 1).wait_send()
-            yr_copy(d, q, d, 2).wait_send()
+                yr_copy(d, q, 2 * d + half, 2).wait_send()
+            for k in range(4):
+                yr_copy(d, q, k, 1).wait_send()
 
     @pl.when(home)
     def _():
@@ -477,8 +497,8 @@
             s2_copy(u).wait_send()
 
     for q in (0, 1):
-        for half in (0, 1):
-            for cond, copy in xr_copies(q, half):
+        for k in range(4):
+            for cond, copy in xr_copies(q, k):
                 pl.when(cond)(copy.wait_send)
 
     @pl.when(jnp.logical_and(is_img, home))
@@ -503,8 +523,8 @@
             buf(1024), buf(256), buf(1024), buf(1024), buf(14 * 64), buf(4 * 64), buf(8 * 64), buf(6 * 64), buf(128),
             pltpu.VMEM((1024, 128), jnp.int32), pltpu.VMEM((8, 1024), jnp.int32),
             dma((4,)), dma((3, 2)), dma((2, 2)), dma((2, 2)), dma((2, 2)), dma((4,)), dma((4,)), dma((2, 6)), dma((2, 6)), dma((2, 14)), dma((2, 14)),
-            dma((16,)), dma((16,)), dma((3,)), dma((3,)), dma((2, 14)), dma((2, 14)), dma((2, 6)), dma((2, 6)),
-            dma((2, 2)), dma((3, 2)), dma((4,)), dma((4,)),
+            dma((16,)), dma((16,)), dma((3,)), dma((3,)), dma((2, 14)), dma((2, 14)), dma((2, 12)), dma((2, 12)),
+            dma((2, 4)), dma((3, 4)), dma((4,)), dma((4,)),
         ],
         compiler_params=pltpu.CompilerParams(collective_id=0, has_side_effects=True, vmem_limit_bytes=67043328 - 600000),
         name="towers",

time: 71.5 us -> 71 us (level)
  no operation moved by 1% of the time
where the time goes in v5:
time: 71 us; the launch traced here: 69.6 us
  Pallas kernels  67.5 us (95%)
  between operations  1.3 us (2%)
  local copies, waits for them, and re-layouts  0.82 us (1%)
    pallas_call x1, Pallas kernels, on_device(): pl.pallas_call(kernel, out_shape=pltpu.VMEM((1, n, d), F32), in_specs=[hb...  67.5 us

profile of v5, /device:TPU:2, one launch (start us, length us, event | category | flops | bytes accessed | tf_op | source)
XLA Modules:
  0.0 69.6 jit_solution(9429804669578782029)
XLA Ops:
  1.3 67.5 %towers.1 = f32[1,128,1152]{2,1,0:T(8,128)S(1)} custom-call(bf16[1,128,1152]{2,1,0:T(8,128)(2,1)} %pooled_hbm.1, f32[1,1152]{1,0:T(1,128)} %gain_hbm.1, bf16[1,1152,1152]{2,1,0:T(8,128)(2,1)} %weight.1, s32[128,128]{1,0:T(8,128)} %bitcast.1, f32[1]{0:T(128)S(6)} %copy.9.log_scale, f32[1]{0:T(128)S(6)} %copy.10.bias), custom_call_target="tpu_custom_call" | custom-call | tf_op jit(solution)/shard_map/towers/pallas_call | solution.py:516
  68.8 0.8 %copy.8 = f32[1,128,1152]{2,1,0:T(8,128)} copy(f32[1,128,1152]{2,1,0:T(8,128)S(1)} %towers.1) | data formatting | bytes 1179648
